TPU v7x, 32 devices: a whole 2x2x4 slice. The times are simulated.
32 devices in a mesh: tok: 8 (over z, x), wid: 4 (over y, core).
Axes of the slice: x: 2, y: 2, z: 4, core: 2. Of those that a mesh axis runs over, the one named last changes fastest.
Arguments:
- acts: bfloat16 [3072, 53248], P('tok', 'wid'), may hold values from -100 to 100
- out_grads: bfloat16 [3072, 16384], P('tok', 'wid'), may hold values from -6 to 6
- test_matrix: bfloat16 [16384, 256], P('wid'), may hold values from -1 to 1
Outputs:
- coeffs: float32 [256, 16384], P('tok', 'wid')
All inputs are finite; a program needn't handle non-finite values.
Results may differ from a plain program's by a relative error of at most 0.01.
Values may be sent and summed in bfloat16 or wider, within the bound.
A program may use at most 64 MiB of HBM per device.

v0:
```python
import functools
import math

import jax
import jax.numpy as jnp
from jax import lax
from jax.experimental import pallas as pl
from jax.experimental.pallas import tpu as pltpu
from jax.sharding import PartitionSpec as P

MESH = pl.DeviceIdType.MESH
F32 = jnp.float32
BF16 = jnp.bfloat16
VMEM_LIMIT = 60 * 1024 * 1024
WAYS = (0, 1)
PIECES = 4


def nt(a, b, precision=None):
    return lax.dot_general(
        a, b, (((1,), (1,)), ((), ())), preferred_element_type=F32, precision=precision
    )


class Ring:
    def __init__(self, n):
        self.n, self.rows, self.cols = n, 4, n // 4
        self.body = self.rows * (self.cols - 1)
        self.tok = lax.axis_index("tok")
        self.pos = self.pos_of(self.tok)

    def pos_of(self, tok):
        r, c = lax.div(tok, self.cols), lax.rem(tok, self.cols)
        odd = lax.rem(r, 2)
        inner = lax.div(c + self.cols - 1, self.cols)
        along = r * (self.cols - 1) + (1 - odd) * (c - 1) + odd * (self.cols - 1 - c)
        back = self.body + self.rows - 1 - r
        return inner * along + (1 - inner) * back

    def tok_of(self, pos):
        last = lax.div(pos, self.body)
        r, k = lax.div(pos, self.cols - 1), lax.rem(pos, self.cols - 1)
        odd = lax.rem(r, 2)
        along = r * self.cols + (1 - odd) * (k + 1) + odd * (self.cols - 1 - k)
        back = (self.rows - 1 - (pos - self.body)) * self.cols
        return (1 - last) * along + last * back

    def at(self, offset):
        return lax.rem(self.pos + offset + 2 * self.n, self.n)

    def neighbours(self):
        return self.tok_of(self.at(1)), self.tok_of(self.at(-1))

    def barrier(self, peers=1):
        sem = pltpu.get_barrier_semaphore()
        me = lax.axis_index("wid")
        for k in range(1, peers):
            other = lax.rem(me + k, peers)
            pl.semaphore_signal(
                sem, inc=1, device_id={"wid": other}, device_id_type=MESH
            )
        for other in self.neighbours():
            pl.semaphore_signal(
                sem, inc=1, device_id={"tok": other}, device_id_type=MESH
            )
        pl.semaphore_wait(sem, 1 + peers)


def wid_sum(m, part, got, mine, out, sems):
    me = lax.axis_index("wid")
    share = part.shape[0] // m

    def lines(index):
        return pl.ds(pl.multiple_of(index * share, 16), share)

    def copy(phase, k):
        other = lax.rem(me + k, m)
        return pltpu.make_async_remote_copy(
            src_ref=mine if phase else part.at[lines(other)],
            dst_ref=out.at[lines(me)] if phase else got.at[k - 1],
            send_sem=sems.at[phase, 0, k - 1],
            recv_sem=sems.at[phase, 1, k - 1],
            device_id={"wid": other},
            device_id_type=MESH,
        )

    for k in range(1, m):
        copy(0, k).start()
    total = part[lines(me), :]
    for k in range(1, m):
        copy(0, k).wait_recv()
        total = total + got[k - 1]
    mine[...] = total.astype(mine.dtype)
    for k in range(1, m):
        copy(1, k).start()
    out[lines(me), :] = total.astype(out.dtype)
    for k in range(1, m):
        copy(0, k).wait_send()
        copy(1, k).wait()


def ring_scatter(ring, term, store, send, recv, send_sems, recv_sems):
    n = ring.n
    dest = ring.neighbours()

    def copy(way, step, piece):
        return pltpu.make_async_remote_copy(
            src_ref=send.at[way, step, piece],
            dst_ref=recv.at[way, step, piece],
            send_sem=send_sems.at[way, step, piece],
            recv_sem=recv_sems.at[way, step, piece],
            device_id={"tok": dest[way]},
            device_id_type=MESH,
        )

    def block(way, step):
        return ring.at(-1 - step) if way == 0 else ring.at(1 + step)

    for piece in range(PIECES):
        for way in WAYS:
            send[way, 0, piece] = term(way, piece, block(way, 0)).astype(BF16)
            copy(way, 0, piece).start()

    def step(s, carry):
        for piece in range(PIECES):
            for way in WAYS:
                own = term(way, piece, block(way, s))
                copy(way, s - 1, piece).wait_recv()
                total = own + recv[way, s - 1, piece].astype(F32)
                send[way, s, piece] = total.astype(BF16)
                copy(way, s, piece).start()
        return carry

    lax.fori_loop(1, n - 1, step, 0)
    for piece in range(PIECES):
        for way in WAYS:
            own = term(way, piece, ring.pos)
            copy(way, n - 2, piece).wait_recv()
            store(way, piece, own + recv[way, n - 2, piece].astype(F32))

    def drain(s, carry):
        for piece in range(PIECES):
            for way in WAYS:
                copy(way, s, piece).wait_send()
        return carry

    lax.fori_loop(0, n - 1, drain, 0)


def sketch_kernel(
    n, m, acts, grads, test, out, part, got, mine, probe_t, wid_sems,
    send, recv, send_sems, recv_sems,
):
    ring = Ring(n)
    width = out.shape[1]
    rows = out.shape[0] // (2 * PIECES)

    def term(way, piece, pos):
        first = (way * PIECES + piece) * rows
        columns = pl.ds(pl.multiple_of(pos * width, 128), width)
        return jnp.dot(
            probe_t[first : first + rows, :], acts[:, columns], preferred_element_type=F32
        )

    def store(way, piece, total):
        first = (way * PIECES + piece) * rows
        out[first : first + rows, :] = total.astype(BF16)

    ring.barrier(m)
    part[...] = jnp.dot(grads[...], test[...], preferred_element_type=F32).T
    wid_sum(m, part, got, mine, probe_t, wid_sems)
    ring_scatter(ring, term, store, send, recv, send_sems, recv_sems)


def gather_kernel(
    n, m, acts, own, out_mixed, out_gram, part, got, mine, full, wid_sems,
    held, send_sems, recv_sems,
):
    tokens = acts.shape[0]
    mixed, gram = part.at[0:tokens], part.at[tokens : part.shape[0]]
    ring = Ring(n)
    width = own.shape[1]
    rows = own.shape[0] // (2 * PIECES)
    half = own.shape[0] // 2
    dest = ring.neighbours()

    def copy(way, step, piece, first=False):
        pos = ring.at(-step) if way == 0 else ring.at(step)
        lines = pl.ds((way * PIECES + piece) * rows, rows)
        return pltpu.make_async_remote_copy(
            src_ref=own.at[lines] if first else held.at[pos, lines],
            dst_ref=held.at[pos, lines],
            send_sem=send_sems.at[way, step, piece],
            recv_sem=recv_sems.at[way, step, piece],
            device_id={"tok": dest[way]},
            device_id_type=MESH,
        )

    def add(way, pos, ref):
        columns = pl.ds(pl.multiple_of(pos * width, 128), width)
        lanes = slice(way * half, (way + 1) * half)
        mixed[:, lanes] += nt(acts[:, columns], ref[lanes, :])

    def add_gram(pos):
        block = held.at[pos]
        gram[...] += nt(block[...], block[...])

    ring.barrier(m)
    for piece in range(PIECES):
        for way in WAYS:
            copy(way, 0, piece, True).start()
    mixed[...] = jnp.zeros_like(mixed)
    gram[...] = nt(own[...], own[...])
    for way in WAYS:
        add(way, ring.pos, own)

    def step(s, carry):
        for piece in range(PIECES):
            for way in WAYS:
                copy(way, s - 1, piece).wait_recv()
                copy(way, s, piece).start()
        for way in WAYS:
            pos = ring.at(-s) if way == 0 else ring.at(s)
            add(way, pos, held.at[pos])
        pl.when(2 * s >= n)(lambda: add_gram(ring.at(s)))
        pl.when(2 * s > n)(lambda: add_gram(ring.at(-s)))
        return carry

    lax.fori_loop(1, n - 1, step, 0)
    for piece in range(PIECES):
        for way in WAYS:
            copy(way, n - 2, piece).wait_recv()
    for way in WAYS:
        pos = ring.at(1 - n) if way == 0 else ring.at(n - 1)
        add(way, pos, held.at[pos])

    add_gram(ring.at(n - 1))
    add_gram(ring.at(1 - n))
    wid_sum(m, part, got, mine, full, wid_sems)
    out_mixed[...] = full[0:tokens, :]
    out_gram[...] = full[tokens : part.shape[0], :]

    def drain(s, carry):
        for piece in range(PIECES):
            for way in WAYS:
                copy(way, s, piece, False).wait_send()
        return carry

    lax.fori_loop(0, n - 1, drain, 0)


def invert(lower, inverse):
    i = lax.broadcasted_iota(jnp.int32, lower.shape, 0)
    j = lax.broadcasted_iota(jnp.int32, lower.shape, 1)
    inverse[...] = jnp.where(i == j, 1.0 / jnp.where(i == j, lower[...], 1.0), 0.0)

    def level(k, carry):
        i_block, j_block = lax.shift_right_logical(i, k), lax.shift_right_logical(j, k)
        same = lax.shift_right_logical(i, k + 1) == lax.shift_right_logical(j, k + 1)
        below = jnp.where(jnp.logical_and(same, i_block > j_block), lower[...], 0.0)
        high = lax.Precision.HIGHEST
        right = jnp.dot(below, inverse[...], precision=high, preferred_element_type=F32)
        inverse[...] -= jnp.dot(
            inverse[...], right, precision=high, preferred_element_type=F32
        )
        return carry

    lax.fori_loop(0, (lower.shape[0] - 1).bit_length(), level, 0)


def factor(gram, rest, upper):
    size = gram.shape[0]
    block = math.gcd(size, 32)
    lane = lax.broadcasted_iota(jnp.int32, (block, size), 1)
    line = lax.broadcasted_iota(jnp.int32, (block, size), 0)
    one_line = lax.broadcasted_iota(jnp.int32, (block, 1), 0)
    rest[...] = gram[...]

    def step(k, carry):
        first = pl.multiple_of(k * block, block)
        rows = rest[pl.ds(first, block), :]
        for j in range(block):
            picked = jnp.where(lane == first + j, rows, 0.0)
            column = jnp.sum(picked, axis=1, keepdims=True)
            ratio = jnp.where(one_line > j, column / column[j : j + 1, :], 0.0)
            rows = rows - ratio * rows[j : j + 1, :]
        diagonal = jnp.sum(
            jnp.where(lane == first + line, rows, 0.0), axis=1, keepdims=True
        )
        rows = jnp.where(lane >= first + line, rows / jnp.sqrt(diagonal), 0.0)
        upper[pl.ds(first, block), :] = rows
        rest[...] -= lax.dot_general(
            rows, rows, (((0,), (0,)), ((), ())),
            precision=lax.Precision.HIGHEST, preferred_element_type=F32,
        )
        return carry

    lax.fori_loop(0, size // block, step, 0)


def coeffs_kernel(
    n, scale, mixed, gram, grads, out, rest, lower, inverse, terms,
    send, recv, send_sems, recv_sems,
):
    ring = Ring(n)
    rows, width = out.shape
    part = width // (2 * PIECES)

    def term(way, piece, pos):
        first = (way * PIECES + piece) * part
        return terms[ring.tok_of(pos), :, first : first + part]

    def store(way, piece, total):
        first = (way * PIECES + piece) * part
        out[:, first : first + part] = total

    ring.barrier()
    factor(gram, rest, inverse)
    lower[...] = inverse[...].T
    invert(lower, inverse)
    proj_t = nt(inverse[...], mixed[...], lax.Precision.HIGHEST).astype(BF16)
    for first in range(0, width, 512 if width % 512 == 0 else width):
        last = min(width, first + 512) if width % 512 == 0 else width
        piece = jnp.dot(proj_t, grads[:, first:last], preferred_element_type=F32)
        terms[:, :, first:last] = (piece * scale).reshape(n, rows, last - first)
    ring_scatter(ring, term, store, send, recv, send_sems, recv_sems)


def call(kernel, outs, scratch, number, *args):
    vmem = pl.BlockSpec(memory_space=pltpu.VMEM)
    return pl.pallas_call(
        kernel,
        out_shape=outs,
        in_specs=[vmem] * len(args),
        out_specs=jax.tree.map(lambda _: vmem, outs),
        scratch_shapes=scratch,
        compiler_params=pltpu.CompilerParams(
            collective_id=number, has_side_effects=True, vmem_limit_bytes=VMEM_LIMIT
        ),
    )(*args)


def sems(n):
    return [pltpu.SemaphoreType.DMA((2, n - 1, PIECES)) for _ in range(2)]


def slots(n, rows, width):
    return [pltpu.VMEM((2, n - 1, PIECES, rows, width), BF16) for _ in range(2)]


def factor_inverse(gram):
    lower = jnp.linalg.cholesky(gram)
    eye_matrix = jnp.eye(gram.shape[0], dtype=F32)
    return lax.linalg.triangular_solve(lower, eye_matrix, left_side=True, lower=True)


def wid_scratch(m, rows, width, dtype):
    return [
        pltpu.VMEM((rows, width), F32),
        pltpu.VMEM((m - 1, rows // m, width), F32),
        pltpu.VMEM((rows // m, width), dtype),
        pltpu.VMEM((rows, width), dtype),
        pltpu.SemaphoreType.DMA((2, 2, m - 1)),
    ]


def ring_shards(n, m, acts, out_grads, test_matrix):
    tokens, hidden = acts.shape
    rank, model = test_matrix.shape[1], out_grads.shape[1]
    width = hidden // n
    struct = jax.ShapeDtypeStruct
    rows_t = call(
        functools.partial(sketch_kernel, n, m),
        struct((rank, width), BF16),
        wid_scratch(m, rank, tokens, BF16)
        + slots(n, rank // (2 * PIECES), width) + sems(n),
        0, acts, out_grads, test_matrix,
    )
    mixed, gram = call(
        functools.partial(gather_kernel, n, m),
        [struct((tokens, rank), F32), struct((rank, rank), F32)],
        wid_scratch(m, tokens + rank, rank, F32)
        + [pltpu.VMEM((n, rank, width), BF16)] + sems(n),
        1, acts, rows_t,
    )
    scale = 1.0 / math.sqrt(tokens * n)
    rows = rank // n
    return call(
        functools.partial(coeffs_kernel, n, scale),
        struct((rows, model), F32),
        [pltpu.VMEM((rank, rank), F32) for _ in range(3)]
        + [pltpu.VMEM((n, rows, model), F32)]
        + slots(n, rows, model // (2 * PIECES)) + sems(n),
        2, mixed, gram, out_grads,
    )


def plain_shards(acts, out_grads, test_matrix):
    partial_probe = jnp.dot(out_grads, test_matrix, preferred_element_type=F32)
    probe = lax.psum(partial_probe, "wid").astype(BF16)
    local_sketch = lax.dot_general(
        acts, probe, (((0,), (0,)), ((), ())), preferred_element_type=F32
    )
    sketch = lax.psum(local_sketch.astype(BF16), "tok")
    gram = lax.psum(
        lax.dot_general(sketch, sketch, (((0,), (0,)), ((), ())), preferred_element_type=F32),
        "wid",
    )
    inverse = factor_inverse(gram)
    mixed = lax.psum(jnp.dot(acts, sketch, preferred_element_type=F32), "wid")
    proj = jnp.dot(mixed, inverse.T, precision=lax.Precision.HIGHEST).astype(BF16)
    scale = 1.0 / math.sqrt(acts.shape[0] * lax.axis_size("tok"))
    term = lax.dot_general(
        proj, out_grads, (((0,), (0,)), ((), ())), preferred_element_type=F32
    )
    return lax.psum_scatter(term * scale, "tok", scatter_dimension=0, tiled=True)


def solution(mesh):
    n, m = mesh.shape["tok"], mesh.shape["wid"]

    def shards(acts, out_grads, test_matrix):
        width, left = divmod(acts.shape[1], n)
        even = acts.shape[0] % (16 * m) == 0 and test_matrix.shape[1] % (16 * m) == 0
        if n % 4 == 0 and n > 4 and m > 1 and even and left == 0 and width % 128 == 0:
            return ring_shards(n, m, acts, out_grads, test_matrix)
        return plain_shards(acts, out_grads, test_matrix)

    return jax.shard_map(
        shards,
        mesh=mesh,
        in_specs=(P("tok", "wid"), P("tok", "wid"), P("wid", None)),
        out_specs=P("tok", "wid"),
        check_vma=False,
    )
```

profile of v0, /device:TPU:0, one launch (start us, length us, event | category | flops | bytes accessed | tf_op | source)
XLA Modules:
  0.0 247.1 jit_solution(15595758242534584597)
XLA Ops:
  0.0 89.0 %shard_map.37.own = bf16[256,1664]{1,0:T(8,128)(2,1)} custom-call(bf16[384,13312]{1,0:T(8,128)(2,1)} %acts.3, bf16[384,4096]{1,0:T(8,128)(2,1)} %grads.3, bf16[4096,256]{1,0:T(8,128)(2,1)} %test.1), custom_call_target="tpu_custom_call" | custom-call | tf_op jit(solution)/shard_map/pallas_call | solution.py:331
  89.1 89.2 %shard_map.38 = (f32[384,256]{1,0:T(8,128)}, f32[256,256]{1,0:T(8,128)}) custom-call(bf16[384,13312]{1,0:T(8,128)(2,1)} %acts.3, bf16[256,1664]{1,0:T(8,128)(2,1)} %shard_map.37.own), custom_call_target="tpu_custom_call" | custom-call | tf_op jit(solution)/shard_map/pallas_call | solution.py:331
  178.3 66.9 %shard_map.39 = f32[32,4096]{1,0:T(8,128)} custom-call(f32[384,256]{1,0:T(8,128)} %get-tuple-element.7.mixed, f32[256,256]{1,0:T(8,128)} %get-tuple-element.8.gram, bf16[384,4096]{1,0:T(8,128)(2,1)} %grads.3), custom_call_target="tpu_custom_call" | custom-call | tf_op jit(solution)/shard_map/pallas_call | solution.py:331
  245.2 1.9 copy.5
where the time goes:
time: 247 us
  Pallas kernels  245 us (99%)
    pallas_call x3, Pallas kernels, call(): pl.pallas_call(kernel, out_shape=outs, in_specs=[vmem] * len(args), out_s...  245 us

commit v1 on v0

v1 whole, which is shorter than its diff:
```python
import functools
import math
import types

import jax
import jax.numpy as jnp
from jax import lax
from jax.experimental import pallas as pl
from jax.experimental.pallas import tpu as pltpu
from jax.sharding import PartitionSpec as P

MESH = pl.DeviceIdType.MESH
F32 = jnp.float32
BF16 = jnp.bfloat16
HIGH = lax.Precision.HIGHEST
VMEM_LIMIT = 60 * 1024 * 1024
LINE = 4
ENDS = 2
PARTS = 2
PIECES = 16
PANELS = 8
GROUPS = 3
SKEW = 3
HOPS = GROUPS * PIECES
LAST = LINE - 1
FILL = SKEW * LAST
REDUCED = HOPS + FILL
SLOTS = HOPS + REDUCED
WAYS = (0, 1)
RING_PIECES = 4


def nt(a, b, precision=None):
    return lax.dot_general(
        a, b, (((1,), (1,)), ((), ())), preferred_element_type=F32, precision=precision
    )


def tn(a, b, precision=None):
    return lax.dot_general(
        a, b, (((0,), (0,)), ((), ())), preferred_element_type=F32, precision=precision
    )


def both(a, b):
    return jnp.logical_and(a, b)


def within(value, first, count):
    return both(value >= first, value < first + count)


class Place:
    def __init__(self, n, m):
        self.n, self.m, self.cols = n, m, n // LINE
        self.tok, self.wid = lax.axis_index("tok"), lax.axis_index("wid")
        self.z, self.x = lax.div(self.tok, self.cols), lax.rem(self.tok, self.cols)
        self.across = self.z * self.cols + 1 - self.x
        self.end = lax.div(self.z, LAST)
        self.is_end = lax.rem(self.z, LAST) == 0

    def along(self, step):
        return lax.rem(self.z + step + LINE, LINE) * self.cols + self.x

    def to_end(self, end):
        return self.z if end else LAST - self.z

    def peer(self, k):
        return lax.rem(self.wid + k, self.m)

    def barrier(self):
        sem = pltpu.get_barrier_semaphore()
        others = [{"wid": self.peer(k)} for k in range(1, self.m)]
        others += [{"tok": self.along(step)} for step in range(1, LINE)]
        others += [{"tok": self.across}]
        for other in others:
            pl.semaphore_signal(sem, inc=1, device_id=other, device_id_type=MESH)
        pl.semaphore_wait(sem, len(others))


def remote(src, dst, sems, index, device):
    return pltpu.make_async_remote_copy(
        src_ref=src,
        dst_ref=dst,
        send_sem=sems[0].at[index],
        recv_sem=sems[1].at[index],
        device_id=device,
        device_id_type=MESH,
    )


def unit_of(end, x, part):
    return (end * 2 + x) * PARTS + part


def shares(place, rows):
    share = rows // place.m
    return lambda index: pl.ds(pl.multiple_of(index * share, 16), share)


def wid_sum(place, part, got, mine, out, sems, finish):
    lines = shares(place, part.shape[0])
    me = place.wid

    def copy(phase, k):
        other = place.peer(k)
        return remote(
            mine if phase else part.at[lines(other)],
            out.at[lines(me)] if phase else got.at[k - 1],
            sems,
            (phase, k - 1),
            {"wid": other},
        )

    for k in range(1, place.m):
        copy(0, k).start()
    total = part[lines(me), :]
    for k in range(1, place.m):
        copy(0, k).wait_recv()
        total = total + got[k - 1]
    total = finish(total).astype(mine.dtype)
    mine[...] = total
    for k in range(1, place.m):
        copy(1, k).start()
    out[lines(me), :] = total
    for k in range(1, place.m):
        copy(0, k).wait_send()
        copy(1, k).wait()


def reduce_sketch(place, acts, probe, terms, line, cross, last, full, line_sems, cross_sems, last_sems):
    x, end = place.x, place.end
    width = terms.shape[-1]

    def compute(unit):
        columns = pl.ds(pl.multiple_of(unit * width, 128), width)
        term = jnp.dot(probe[...], acts[:, columns], preferred_element_type=F32)
        terms[unit] = term.astype(BF16).reshape(terms.shape[1:])

    def order(i):
        first = lax.div(i, 4)
        side = jnp.where(first == 0, 1 - x, x)
        k = lax.rem(i, 4)
        return unit_of(lax.rem(k, 2), side, 1 - lax.div(k, 2))

    def spot(end_, k):
        group, piece = lax.div(k, PIECES), lax.rem(k, PIECES)
        side = jnp.where(group == 0, 1 - x, x)
        part = jnp.where(group == GROUPS - 1, 0, 1)
        return group, piece, unit_of(end_, side, part)

    def line_copy(way, k, src):
        step = 1 if way else -1
        return remote(src, line.at[way, k], line_sems, (way, k), {"tok": place.along(step)})

    def cross_copy(way, piece):
        unit = unit_of(way, 1 - x, 0)
        return remote(
            terms.at[unit, piece], cross.at[way, piece], cross_sems, (way, piece),
            {"tok": place.across},
        )

    def last_copy(piece):
        return remote(
            line.at[end, piece], last.at[piece], last_sems, piece, {"tok": place.across}
        )

    def hop(way, k):
        pos = place.to_end(way)
        group, piece, unit = spot(way, k)

        @pl.when(pos == 0)
        def _():
            line_copy(way, k, terms.at[unit, piece]).start()

        @pl.when(pos > 0)
        def _():
            line_copy(way, k, line.at[way, k]).wait_recv()

        @pl.when(both(pos > 0, group != 1))
        def _():
            total = line[way, k].astype(F32) + terms[unit, piece].astype(F32)
            line[way, k] = total.astype(BF16)

        @pl.when(both(both(pos > 0, pos < LAST), group == 1))
        def _():
            total = line[way, k].astype(F32) + terms[unit, piece].astype(F32)
            line[way, k] = total.astype(BF16)

        @pl.when(both(pos > 0, pos < LAST))
        def _():
            line_copy(way, k, line.at[way, k]).start()

        @pl.when(both(pos == LAST, group == GROUPS - 1))
        def _():
            full[unit, piece] = line[way, k]

    lax.fori_loop(0, 3, lambda i, c: (compute(order(i)), c)[1], 0)

    def slot(s):
        @pl.when(s < 2 * PIECES)
        def _():
            cross_copy(lax.div(s, PIECES), lax.rem(s, PIECES)).start()

        for way in WAYS:
            k = s - SKEW * place.to_end(way)
            pl.when(within(k, 0, HOPS))(functools.partial(hop, way, k))

        pl.when(within(s, 0, 5))(lambda: compute(order(s + 3)))

        @pl.when(within(s, 2 * PIECES - 2, PIECES))
        def _():
            piece = s - (2 * PIECES - 2)
            for way in WAYS:
                cross_copy(way, piece).wait_recv()
                unit = unit_of(way, x, 0)
                total = terms[unit, piece].astype(F32) + cross[way, piece].astype(F32)
                terms[unit, piece] = total.astype(BF16)

        @pl.when(both(place.is_end, within(s, 2 * PIECES - 3, PIECES)))
        def _():
            last_copy(s - (2 * PIECES - 3)).start()

        @pl.when(both(place.is_end, within(s, REDUCED - PIECES, PIECES)))
        def _():
            piece = s - (REDUCED - PIECES)
            last_copy(piece).wait_recv()
            unit = unit_of(end, x, 1)
            total = line[end, PIECES + piece].astype(F32) + last[piece].astype(F32)
            total = total + terms[unit, piece].astype(F32)
            full[unit, piece] = total.astype(BF16)

    def drain():
        for way in WAYS:
            sent = place.to_end(way) < LAST

            @pl.when(sent)
            def _():
                def one(k, carry):
                    line_copy(way, k, line.at[way, k]).wait_send()
                    return carry

                lax.fori_loop(0, HOPS, one, 0)

        def one(k, carry):
            for way in WAYS:
                cross_copy(way, k).wait_send()
            pl.when(place.is_end)(lambda: last_copy(k).wait_send())
            return carry

        lax.fori_loop(0, PIECES, one, 0)

    return slot, drain


class Gram:
    def __init__(self, place, part, got, share, crossed, ends, mine, gram, sems):
        self.place, self.part, self.got, self.share = place, part, got, share
        self.crossed, self.ends, self.mine, self.gram = crossed, ends, mine, gram
        self.wid_sems, self.cross_sems, self.end_sems = sems
        self.lines = shares(place, gram.shape[0])

    def first(self, k):
        other = self.place.peer(k)
        return remote(
            self.part.at[self.lines(other)], self.got.at[k - 1], self.wid_sems, (0, k - 1),
            {"wid": other},
        )

    def over_x(self):
        return remote(
            self.share, self.crossed, self.cross_sems, 0, {"tok": self.place.across}
        )

    def over_z(self, step, end):
        send, recv = self.end_sems
        return pltpu.make_async_remote_copy(
            src_ref=self.ends.at[end],
            dst_ref=self.ends.at[end],
            send_sem=send.at[step - 1],
            recv_sem=recv.at[end],
            device_id={"tok": self.place.along(step)},
            device_id_type=MESH,
        )

    def spread(self, k):
        return remote(
            self.mine, self.gram.at[self.lines(self.place.wid)], self.wid_sems, (1, k - 1),
            {"wid": self.place.peer(k)},
        )

    def start(self, full):
        @pl.when(self.place.is_end)
        def _():
            rank, width = self.part.shape[0], full.shape[-1]
            unit = unit_of(self.place.end, self.place.x, 0)
            a = full[unit].reshape(rank, width)
            b = full[unit + 1].reshape(rank, width)
            self.part[...] = nt(a, a) + nt(b, b)
            for k in range(1, self.place.m):
                self.first(k).start()

    def cross(self):
        @pl.when(self.place.is_end)
        def _():
            total = self.part[self.lines(self.place.wid), :]
            for k in range(1, self.place.m):
                self.first(k).wait_recv()
                total = total + self.got[k - 1]
            self.share[...] = total
            self.over_x().start()

    def along(self):
        @pl.when(self.place.is_end)
        def _():
            self.over_x().wait_recv()
            self.ends[self.place.end] = self.share[...] + self.crossed[...]
            for step in range(1, LINE):
                self.over_z(step, self.place.end).start()

    def gather(self):
        for end in range(ENDS):
            @pl.when(self.place.z != end * LAST)
            def _():
                self.over_z(1, end).wait_recv()

        total = self.ends[0] + self.ends[1]
        self.mine[...] = total
        for k in range(1, self.place.m):
            self.spread(k).start()
        self.gram[self.lines(self.place.wid), :] = total

    def finish(self):
        for k in range(1, self.place.m):
            self.spread(k).wait_recv()

    def drain(self):
        @pl.when(self.place.is_end)
        def _():
            for k in range(1, self.place.m):
                self.first(k).wait_send()
            self.over_x().wait_send()
            for step in range(1, LINE):
                self.over_z(step, self.place.end).wait_send()

        for k in range(1, self.place.m):
            self.spread(k).wait_send()


def gather_sketch(place, acts, full, mixed, gram, rest, lower, inverse, line_sems, forward_sems, swap_sems):
    x, end = place.x, place.end
    rank, width = rest.shape[0], full.shape[-1]
    panel = rank // PANELS
    levels = (rank - 1).bit_length()
    solve_at = FILL + 17
    invert_at = solve_at + 2 * PANELS

    def spot(end_, k):
        group, piece = lax.div(k, PIECES), lax.rem(k, PIECES)
        side = jnp.where(group == GROUPS - 1, 1 - x, x)
        part = jnp.where(group == 0, 0, 1)
        return group, piece, unit_of(end_, side, part)

    def copy(unit, piece, sems, index, device):
        block = full.at[unit, piece]
        return remote(block, block, sems, index, {"tok": device})

    def line_copy(way, k):
        group, piece, unit = spot(way, k)
        return copy(unit, piece, line_sems, (way, k), place.along(-1 if way else 1))

    def forward_copy(way, piece):
        return copy(unit_of(way, x, 0), piece, forward_sems, (way, piece), place.across)

    def swap_copy(piece):
        return copy(unit_of(end, x, 1), piece, swap_sems, piece, place.across)

    def hop(way, k):
        pos = place.to_end(1 - way)
        group, piece, unit = spot(way, k)

        @pl.when(pos > 0)
        def _():
            line_copy(way, k).wait_recv()

        @pl.when(both(pos == 0, group == GROUPS - 1))
        def _():
            swap_copy(piece).wait_recv()

        @pl.when(pos < LAST)
        def _():
            line_copy(way, k).start()

    def add(unit):
        columns = pl.ds(pl.multiple_of(unit * width, 128), width)
        mixed[...] += nt(acts[:, columns], full[unit].reshape(rank, width))

    mixed[...] = jnp.zeros_like(mixed)

    def slot(s):
        @pl.when(both(place.is_end, within(s, 0, PIECES)))
        def _():
            swap_copy(s).start()

        for way in WAYS:
            k = s - SKEW * place.to_end(1 - way)
            pl.when(within(k, 0, HOPS))(functools.partial(hop, way, k))
            sent = s - FILL - way * PIECES
            pl.when(within(sent, 0, PIECES))(lambda: forward_copy(way, sent).start())
            came = sent - 4
            pl.when(within(came, 0, PIECES))(lambda: forward_copy(way, came).wait_recv())

        pl.when(s == FILL)(lambda: gram.start(full))
        pl.when(s == FILL + 4)(gram.cross)
        pl.when(s == FILL + 7)(gram.along)
        pl.when(s == FILL + 12)(gram.gather)

        @pl.when(s == solve_at - 1)
        def _():
            gram.finish()
            rest[...] = gram.gram[...]

        solve = s - solve_at
        for half in range(2):
            pl.when(both(within(solve, 0, 2 * PANELS), lax.rem(solve, 2) == half))(
                lambda: factor_panel(lax.div(solve, 2), half, panel, rest, inverse)
            )

        @pl.when(s == invert_at)
        def _():
            lower[...] = inverse[...].T
            start_invert(lower, inverse)

        pl.when(within(s, invert_at, levels))(
            lambda: invert_level(s - invert_at, lower, inverse)
        )
        for way in WAYS:
            pl.when(s == PIECES + FILL + way)(lambda: add(unit_of(way, x, 0)))
            pl.when(s == 2 * PIECES + FILL + way)(lambda: add(unit_of(way, x, 1)))
            pl.when(s == (way + 1) * PIECES + FILL + 4)(lambda: add(unit_of(way, 1 - x, 0)))

    def finish():
        for way in WAYS:
            add(unit_of(way, 1 - x, 1))

    def drain():
        for way in WAYS:
            @pl.when(place.to_end(1 - way) < LAST)
            def _():
                def one(k, carry):
                    line_copy(way, k).wait_send()
                    return carry

                lax.fori_loop(0, HOPS, one, 0)

        def one(k, carry):
            for way in WAYS:
                forward_copy(way, k).wait_send()
            pl.when(place.is_end)(lambda: swap_copy(k).wait_send())
            return carry

        lax.fori_loop(0, PIECES, one, 0)

    return slot, finish, drain


def factor_panel(k, half, block, rest, upper):
    size = rest.shape[0]
    lane = lax.broadcasted_iota(jnp.int32, (block, size), 1)
    line = lax.broadcasted_iota(jnp.int32, (block, size), 0)
    one_line = lax.broadcasted_iota(jnp.int32, (block, 1), 0)
    first = pl.multiple_of(k * block, block)
    rows = rest[pl.ds(first, block), :]
    for j in range(half * block // 2, (half + 1) * block // 2):
        picked = jnp.where(lane == first + j, rows, 0.0)
        column = jnp.sum(picked, axis=1, keepdims=True)
        ratio = jnp.where(one_line > j, column / column[j : j + 1, :], 0.0)
        rows = rows - ratio * rows[j : j + 1, :]
    if half == 0:
        rest[pl.ds(first, block), :] = rows
        return
    diagonal = jnp.sum(
        jnp.where(lane == first + line, rows, 0.0), axis=1, keepdims=True
    )
    rows = jnp.where(lane >= first + line, rows / jnp.sqrt(diagonal), 0.0)
    upper[pl.ds(first, block), :] = rows
    rest[...] -= tn(rows, rows, HIGH)


def start_invert(lower, inverse):
    i = lax.broadcasted_iota(jnp.int32, lower.shape, 0)
    j = lax.broadcasted_iota(jnp.int32, lower.shape, 1)
    inverse[...] = jnp.where(i == j, 1.0 / jnp.where(i == j, lower[...], 1.0), 0.0)


def invert_level(k, lower, inverse):
    i = lax.broadcasted_iota(jnp.int32, lower.shape, 0)
    j = lax.broadcasted_iota(jnp.int32, lower.shape, 1)
    i_block, j_block = lax.shift_right_logical(i, k), lax.shift_right_logical(j, k)
    same = lax.shift_right_logical(i, k + 1) == lax.shift_right_logical(j, k + 1)
    below = jnp.where(jnp.logical_and(same, i_block > j_block), lower[...], 0.0)
    right = jnp.dot(below, inverse[...], precision=HIGH, preferred_element_type=F32)
    inverse[...] -= jnp.dot(inverse[...], right, precision=HIGH, preferred_element_type=F32)


class Ring:
    def __init__(self, n):
        self.n, self.rows, self.cols = n, LINE, n // LINE
        self.body = self.rows * (self.cols - 1)
        self.tok = lax.axis_index("tok")
        self.pos = self.pos_of(self.tok)

    def pos_of(self, tok):
        r, c = lax.div(tok, self.cols), lax.rem(tok, self.cols)
        odd = lax.rem(r, 2)
        inner = lax.div(c + self.cols - 1, self.cols)
        along = r * (self.cols - 1) + (1 - odd) * (c - 1) + odd * (self.cols - 1 - c)
        back = self.body + self.rows - 1 - r
        return inner * along + (1 - inner) * back

    def tok_of(self, pos):
        last = lax.div(pos, self.body)
        r, k = lax.div(pos, self.cols - 1), lax.rem(pos, self.cols - 1)
        odd = lax.rem(r, 2)
        along = r * self.cols + (1 - odd) * (k + 1) + odd * (self.cols - 1 - k)
        back = (self.rows - 1 - (pos - self.body)) * self.cols
        return (1 - last) * along + last * back

    def at(self, offset):
        return lax.rem(self.pos + offset + 2 * self.n, self.n)

    def neighbours(self):
        return self.tok_of(self.at(1)), self.tok_of(self.at(-1))


def ring_scatter(ring, term, store, send, recv, sems):
    n = ring.n
    dest = ring.neighbours()

    def copy(way, step, piece):
        return remote(
            send.at[way, step, piece], recv.at[way, step, piece], sems, (way, step, piece),
            {"tok": dest[way]},
        )

    def block(way, step):
        return ring.at(-1 - step) if way == 0 else ring.at(1 + step)

    for piece in range(RING_PIECES):
        for way in WAYS:
            send[way, 0, piece] = term(way, piece, block(way, 0)).astype(BF16)
            copy(way, 0, piece).start()

    def step(s, carry):
        for piece in range(RING_PIECES):
            for way in WAYS:
                own = term(way, piece, block(way, s))
                copy(way, s - 1, piece).wait_recv()
                total = own + recv[way, s - 1, piece].astype(F32)
                send[way, s, piece] = total.astype(BF16)
                copy(way, s, piece).start()
        return carry

    lax.fori_loop(1, n - 1, step, 0)
    for piece in range(RING_PIECES):
        for way in WAYS:
            own = term(way, piece, ring.pos)
            copy(way, n - 2, piece).wait_recv()
            store(way, piece, own + recv[way, n - 2, piece].astype(F32))

    def drain(s, carry):
        for piece in range(RING_PIECES):
            for way in WAYS:
                copy(way, s, piece).wait_send()
        return carry

    lax.fori_loop(0, n - 1, drain, 0)


def coeffs(place, proj, grads, out, terms, send, recv, sems, scale):
    ring = Ring(place.n)
    rows, width = out.shape
    part = width // (2 * RING_PIECES)

    def term(way, piece, pos):
        first = (way * RING_PIECES + piece) * part
        return terms[ring.tok_of(pos), :, first : first + part]

    def store(way, piece, total):
        first = (way * RING_PIECES + piece) * part
        out[:, first : first + part] = total

    for first in range(0, width, part):
        last = first + part
        piece = tn(proj[...], grads[:, first:last])
        terms[:, :, first:last] = (piece * scale).reshape(place.n, rows, part)
    ring_scatter(ring, term, store, send, recv, sems)


def kernel(n, m, scale, names, acts_in, grads_in, test_in, out, *refs):
    s = types.SimpleNamespace(**dict(zip(names, refs)))
    place = Place(n, m)
    loads = [
        pltpu.make_async_copy(src, dst, s.load_sems.at[i])
        for i, (src, dst) in enumerate(
            ((grads_in, s.grads), (test_in, s.test), (acts_in, s.acts))
        )
    ]
    for load in loads:
        load.start()
    place.barrier()
    loads[0].wait()
    loads[1].wait()
    s.probe_part[...] = jnp.dot(s.grads[...], s.test[...], preferred_element_type=F32).T
    wid_sum(
        place, s.probe_part, s.probe_got, s.probe_mine, s.probe,
        (s.probe_send, s.probe_recv), lambda total: total,
    )
    loads[2].wait()
    reduce_slot, drain_reduce = reduce_sketch(
        place, s.acts, s.probe, s.terms, s.line, s.cross, s.last, s.full,
        (s.line_send, s.line_recv), (s.cross_send, s.cross_recv), (s.last_send, s.last_recv),
    )
    gram = Gram(
        place, s.gram_part, s.gram_got, s.gram_share, s.gram_cross, s.gram_ends,
        s.gram_mine, s.gram,
        (
            (s.gram_send, s.gram_recv), (s.gram_x_send, s.gram_x_recv),
            (s.gram_z_send, s.gram_z_recv),
        ),
    )
    gather_slot, finish_gather, drain_gather = gather_sketch(
        place, s.acts, s.full, s.mixed, gram, s.rest, s.lower, s.inverse,
        (s.back_send, s.back_recv), (s.forward_send, s.forward_recv),
        (s.swap_send, s.swap_recv),
    )

    def slot(i, carry):
        reduce_slot(i)
        gather_slot(i - HOPS)
        return carry

    lax.fori_loop(0, SLOTS, slot, 0)
    finish_gather()
    wid_sum(
        place, s.mixed, s.mixed_got, s.proj_mine, s.proj, (s.mixed_send, s.mixed_recv),
        lambda total: nt(total, s.inverse[...], HIGH),
    )
    coeffs(
        place, s.proj, s.grads, out, s.out_terms, s.ring_from, s.ring_to,
        (s.ring_send, s.ring_recv), scale,
    )
    drain_reduce()
    drain_gather()
    gram.drain()


def scratch_of(n, m, tokens, hidden, rank, model):
    units = ENDS * 2 * PARTS
    block = (rank // PIECES, hidden // units)
    vmem, dma = pltpu.VMEM, pltpu.SemaphoreType.DMA
    rows = rank // n
    part = model // (2 * RING_PIECES)

    def pair(name, shape):
        return {name + "_send": dma(shape), name + "_recv": dma(shape)}

    return {
        "acts": vmem((tokens, hidden), BF16),
        "grads": vmem((tokens, model), BF16),
        "test": vmem((model, rank), BF16),
        "load_sems": dma((3,)),
        "probe_part": vmem((rank, tokens), F32),
        "probe_got": vmem((m - 1, rank // m, tokens), F32),
        "probe_mine": vmem((rank // m, tokens), BF16),
        "probe": vmem((rank, tokens), BF16),
        **pair("probe", (2, m - 1)),
        "terms": vmem((units, PIECES, *block), BF16),
        "line": vmem((ENDS, HOPS, *block), BF16),
        "cross": vmem((ENDS, PIECES, *block), BF16),
        "last": vmem((PIECES, *block), BF16),
        "full": vmem((units, PIECES, *block), BF16),
        **pair("line", (ENDS, HOPS)),
        **pair("cross", (ENDS, PIECES)),
        **pair("last", (PIECES,)),
        "gram_part": vmem((rank, rank), F32),
        "gram_got": vmem((m - 1, rank // m, rank), F32),
        "gram_share": vmem((rank // m, rank), F32),
        "gram_cross": vmem((rank // m, rank), F32),
        "gram_ends": vmem((ENDS, rank // m, rank), F32),
        "gram_mine": vmem((rank // m, rank), F32),
        "gram": vmem((rank, rank), F32),
        **pair("gram", (2, m - 1)),
        **pair("gram_x", (1,)),
        "gram_z_send": dma((LAST,)),
        "gram_z_recv": dma((ENDS,)),
        "mixed": vmem((tokens, rank), F32),
        "rest": vmem((rank, rank), F32),
        "lower": vmem((rank, rank), F32),
        "inverse": vmem((rank, rank), F32),
        **pair("back", (ENDS, HOPS)),
        **pair("forward", (ENDS, PIECES)),
        **pair("swap", (PIECES,)),
        "mixed_got": vmem((m - 1, tokens // m, rank), F32),
        "proj_mine": vmem((tokens // m, rank), BF16),
        "proj": vmem((tokens, rank), BF16),
        **pair("mixed", (2, m - 1)),
        "out_terms": vmem((n, rows, model), F32),
        "ring_from": vmem((2, n - 1, RING_PIECES, rows, part), BF16),
        "ring_to": vmem((2, n - 1, RING_PIECES, rows, part), BF16),
        **pair("ring", (2, n - 1, RING_PIECES)),
    }


def line_shards(n, m, acts, out_grads, test_matrix):
    tokens, hidden = acts.shape
    rank, model = test_matrix.shape[1], out_grads.shape[1]
    scratch = scratch_of(n, m, tokens, hidden, rank, model)
    scale = 1.0 / math.sqrt(tokens * n)
    return pl.pallas_call(
        functools.partial(kernel, n, m, scale, tuple(scratch)),
        out_shape=jax.ShapeDtypeStruct((rank // n, model), F32),
        in_specs=[pl.BlockSpec(memory_space=pl.ANY)] * 3,
        out_specs=pl.BlockSpec(memory_space=pltpu.VMEM),
        scratch_shapes=list(scratch.values()),
        compiler_params=pltpu.CompilerParams(
            collective_id=0, has_side_effects=True, vmem_limit_bytes=VMEM_LIMIT
        ),
    )(acts, out_grads, test_matrix)


def factor_inverse(gram):
    lower = jnp.linalg.cholesky(gram)
    eye_matrix = jnp.eye(gram.shape[0], dtype=F32)
    return lax.linalg.triangular_solve(lower, eye_matrix, left_side=True, lower=True)


def plain_shards(acts, out_grads, test_matrix):
    partial_probe = jnp.dot(out_grads, test_matrix, preferred_element_type=F32)
    probe = lax.psum(partial_probe, "wid").astype(BF16)
    local_sketch = lax.dot_general(
        acts, probe, (((0,), (0,)), ((), ())), preferred_element_type=F32
    )
    sketch = lax.psum(local_sketch.astype(BF16), "tok")
    gram = lax.psum(
        lax.dot_general(sketch, sketch, (((0,), (0,)), ((), ())), preferred_element_type=F32),
        "wid",
    )
    inverse = factor_inverse(gram)
    mixed = lax.psum(jnp.dot(acts, sketch, preferred_element_type=F32), "wid")
    proj = jnp.dot(mixed, inverse.T, precision=lax.Precision.HIGHEST).astype(BF16)
    scale = 1.0 / math.sqrt(acts.shape[0] * lax.axis_size("tok"))
    term = lax.dot_general(
        proj, out_grads, (((0,), (0,)), ((), ())), preferred_element_type=F32
    )
    return lax.psum_scatter(term * scale, "tok", scatter_dimension=0, tiled=True)


def solution(mesh):
    n, m = mesh.shape["tok"], mesh.shape["wid"]

    def shards(acts, out_grads, test_matrix):
        tokens, hidden = acts.shape
        model, rank = test_matrix.shape
        fits = (
            n == 2 * LINE
            and m > 1
            and tokens % (16 * m) == 0
            and rank % (16 * m) == 0
            and rank % (16 * PIECES) == 0
            and rank % (16 * n) == 0
            and rank <= 512
            and hidden % (ENDS * 2 * PARTS * 128) == 0
            and model % (2 * RING_PIECES * 128) == 0
            and (tokens * hidden + 2 * rank * hidden) * 2 < VMEM_LIMIT // 2
        )
        if fits:
            return line_shards(n, m, acts, out_grads, test_matrix)
        return plain_shards(acts, out_grads, test_matrix)

    return jax.shard_map(
        shards,
        mesh=mesh,
        in_specs=(P("tok", "wid"), P("tok", "wid"), P("wid", None)),
        out_specs=P("tok", "wid"),
        check_vma=False,
    )
```

time: 247 us -> 209 us (0.85)
  Pallas kernels: 245 us -> 207 us
    pallas_call x3 -> x1, Pallas kernels: 245 us -> 207 us  [line_shards(): pl.pallas_call(functools.partial(kernel, n, m, scale, tuple(scratch)), ou...]
where the time goes in v1:
time: 209 us; the launch traced here: 208 us
  Pallas kernels  207 us (99%)
    pallas_call x1, Pallas kernels, line_shards(): pl.pallas_call(functools.partial(kernel, n, m, scale, tuple(scratch)), ou...  207 us

profile of v1, /device:TPU:0, one launch (start us, length us, event | category | flops | bytes accessed | tf_op | source)
XLA Modules:
  0.0 208.4 jit_solution(13533930953724574324)
XLA Ops:
  0.0 206.5 %shard_map.37 = f32[32,4096]{1,0:T(8,128)} custom-call(bf16[384,13312]{1,0:T(8,128)(2,1)} %acts_in.1, bf16[384,4096]{1,0:T(8,128)(2,1)} %grads_in.1, bf16[4096,256]{1,0:T(8,128)(2,1)} %test_in.1), custom_call_target="tpu_custom_call" | custom-call | tf_op jit(solution)/shard_map/pallas_call | solution.py:720
  206.5 1.9 copy.5

commit v2 on v1

--- a/solution.py
+++ b/solution.py
@@ -19,8 +19,10 @@
 PARTS = 2
 PIECES = 16
 PANELS = 8
+TURNS = 2
+STEP = 8
 GROUPS = 3
-SKEW = 3
+SKEW = 5
 HOPS = GROUPS * PIECES
 LAST = LINE - 1
 FILL = SKEW * LAST
@@ -138,10 +140,10 @@
         terms[unit] = term.astype(BF16).reshape(terms.shape[1:])
 
     def order(i):
-        first = lax.div(i, 4)
-        side = jnp.where(first == 0, 1 - x, x)
+        side = jnp.where(lax.div(i, 4) == 0, 1 - x, x)
         k = lax.rem(i, 4)
-        return unit_of(lax.rem(k, 2), side, 1 - lax.div(k, 2))
+        own = lax.div(k, 2)
+        return unit_of(lax.rem(1 - end + own, 2), side, 1 - lax.rem(k, 2))
 
     def spot(end_, k):
         group, piece = lax.div(k, PIECES), lax.rem(k, PIECES)
@@ -195,18 +197,19 @@
         def _():
             full[unit, piece] = line[way, k]
 
-    lax.fori_loop(0, 3, lambda i, c: (compute(order(i)), c)[1], 0)
+    compute(order(0))
 
     def slot(s):
-        @pl.when(s < 2 * PIECES)
-        def _():
-            cross_copy(lax.div(s, PIECES), lax.rem(s, PIECES)).start()
-
         for way in WAYS:
             k = s - SKEW * place.to_end(way)
             pl.when(within(k, 0, HOPS))(functools.partial(hop, way, k))
 
-        pl.when(within(s, 0, 5))(lambda: compute(order(s + 3)))
+        pl.when(within(s, 0, 7))(lambda: compute(order(s + 1)))
+
+        @pl.when(s < 2 * PIECES)
+        def _():
+            first = lax.rem(1 - end + lax.div(s, PIECES), 2)
+            cross_copy(first, lax.rem(s, PIECES)).start()
 
         @pl.when(within(s, 2 * PIECES - 2, PIECES))
         def _():
@@ -272,16 +275,10 @@
             self.share, self.crossed, self.cross_sems, 0, {"tok": self.place.across}
         )
 
-    def over_z(self, step, end):
-        send, recv = self.end_sems
-        return pltpu.make_async_remote_copy(
-            src_ref=self.ends.at[end],
-            dst_ref=self.ends.at[end],
-            send_sem=send.at[step - 1],
-            recv_sem=recv.at[end],
-            device_id={"tok": self.place.along(step)},
-            device_id_type=MESH,
-        )
+    def over_z(self, end):
+        block = self.ends.at[end]
+        step = -1 if end else 1
+        return remote(block, block, self.end_sems, end, {"tok": self.place.along(step)})
 
     def spread(self, k):
         return remote(
@@ -315,15 +312,19 @@
         def _():
             self.over_x().wait_recv()
             self.ends[self.place.end] = self.share[...] + self.crossed[...]
-            for step in range(1, LINE):
-                self.over_z(step, self.place.end).start()
+            for end in range(ENDS):
+                pl.when(self.place.end == end)(lambda: self.over_z(end).start())
+
+    def relay(self, step):
+        for end in range(ENDS):
+            @pl.when(self.place.to_end(1 - end) == step)
+            def _():
+                self.over_z(end).wait_recv()
+                if step < LAST:
+                    self.over_z(end).start()
 
     def gather(self):
-        for end in range(ENDS):
-            @pl.when(self.place.z != end * LAST)
-            def _():
-                self.over_z(1, end).wait_recv()
-
+        self.relay(LAST)
         total = self.ends[0] + self.ends[1]
         self.mine[...] = total
         for k in range(1, self.place.m):
@@ -340,20 +341,19 @@
             for k in range(1, self.place.m):
                 self.first(k).wait_send()
             self.over_x().wait_send()
-            for step in range(1, LINE):
-                self.over_z(step, self.place.end).wait_send()
-
+
+        for end in range(ENDS):
+            pl.when(self.place.to_end(1 - end) < LAST)(
+                lambda: self.over_z(end).wait_send()
+            )
         for k in range(1, self.place.m):
             self.spread(k).wait_send()
 
 
-def gather_sketch(place, acts, full, mixed, gram, rest, lower, inverse, line_sems, forward_sems, swap_sems):
+def gather_sketch(place, acts, full, mixed, gram, rest, right, inverse, line_sems, forward_sems, swap_sems):
     x, end = place.x, place.end
     rank, width = rest.shape[0], full.shape[-1]
-    panel = rank // PANELS
-    levels = (rank - 1).bit_length()
-    solve_at = FILL + 17
-    invert_at = solve_at + 2 * PANELS
+    solve_at = FILL + 29
 
     def spot(end_, k):
         group, piece = lax.div(k, PIECES), lax.rem(k, PIECES)
@@ -407,37 +407,32 @@
             pl.when(within(k, 0, HOPS))(functools.partial(hop, way, k))
             sent = s - FILL - way * PIECES
             pl.when(within(sent, 0, PIECES))(lambda: forward_copy(way, sent).start())
-            came = sent - 4
+            came = sent - 12
             pl.when(within(came, 0, PIECES))(lambda: forward_copy(way, came).wait_recv())
 
         pl.when(s == FILL)(lambda: gram.start(full))
         pl.when(s == FILL + 4)(gram.cross)
-        pl.when(s == FILL + 7)(gram.along)
-        pl.when(s == FILL + 12)(gram.gather)
+        pl.when(s == FILL + 9)(gram.along)
+        for step in range(1, LAST):
+            pl.when(s == FILL + 9 + 5 * step)(lambda: gram.relay(step))
+        pl.when(s == FILL + 9 + 5 * LAST)(gram.gather)
 
         @pl.when(s == solve_at - 1)
         def _():
             gram.finish()
-            rest[...] = gram.gram[...]
+            start_solve(gram.gram, rest, right)
 
         solve = s - solve_at
-        for half in range(2):
-            pl.when(both(within(solve, 0, 2 * PANELS), lax.rem(solve, 2) == half))(
-                lambda: factor_panel(lax.div(solve, 2), half, panel, rest, inverse)
+        for part in range(TURNS):
+            mine = both(within(solve, 0, TURNS * PANELS), lax.rem(solve, TURNS) == part)
+            pl.when(mine)(
+                lambda: solve_part(lax.div(solve, TURNS), part, rest, right, inverse)
             )
 
-        @pl.when(s == invert_at)
-        def _():
-            lower[...] = inverse[...].T
-            start_invert(lower, inverse)
-
-        pl.when(within(s, invert_at, levels))(
-            lambda: invert_level(s - invert_at, lower, inverse)
-        )
         for way in WAYS:
             pl.when(s == PIECES + FILL + way)(lambda: add(unit_of(way, x, 0)))
             pl.when(s == 2 * PIECES + FILL + way)(lambda: add(unit_of(way, x, 1)))
-            pl.when(s == (way + 1) * PIECES + FILL + 4)(lambda: add(unit_of(way, 1 - x, 0)))
+            pl.when(s == (way + 1) * PIECES + FILL + 12)(lambda: add(unit_of(way, 1 - x, 0)))
 
     def finish():
         for way in WAYS:
@@ -464,43 +459,62 @@
     return slot, finish, drain
 
 
-def factor_panel(k, half, block, rest, upper):
+def start_solve(gram, rest, right):
+    i = lax.broadcasted_iota(jnp.int32, rest.shape, 0)
+    j = lax.broadcasted_iota(jnp.int32, rest.shape, 1)
+    rest[...] = gram[...]
+    right[...] = jnp.where(i == j, 1.0, 0.0)
+
+
+def solve_part(k, part, rest, right, inverse):
     size = rest.shape[0]
+    block = size // PANELS
     lane = lax.broadcasted_iota(jnp.int32, (block, size), 1)
     line = lax.broadcasted_iota(jnp.int32, (block, size), 0)
     one_line = lax.broadcasted_iota(jnp.int32, (block, 1), 0)
     first = pl.multiple_of(k * block, block)
-    rows = rest[pl.ds(first, block), :]
-    for j in range(half * block // 2, (half + 1) * block // 2):
-        picked = jnp.where(lane == first + j, rows, 0.0)
-        column = jnp.sum(picked, axis=1, keepdims=True)
-        ratio = jnp.where(one_line > j, column / column[j : j + 1, :], 0.0)
-        rows = rows - ratio * rows[j : j + 1, :]
-    if half == 0:
-        rest[pl.ds(first, block), :] = rows
+    lines = pl.ds(first, block)
+    rows, side = rest[lines, :], right[lines, :]
+    count = block // TURNS
+    for start in range(part * count, (part + 1) * count, STEP):
+        pivots = range(start, start + STEP)
+        columns = [
+            jnp.sum(jnp.where(lane == first + j, rows, 0.0), axis=1, keepdims=True)
+            for j in pivots
+        ]
+        done = []
+        for c, j in enumerate(pivots):
+            column, later = columns[c], columns[c + 1 :]
+            one = slice(j, j + 1)
+            top, beside = rows[one, :], side[one, :]
+            heads = [other[one, :] for other in later]
+            for ratio, its_top, its_side, its_heads in done:
+                e = len(its_heads) - len(later) - 1
+                column = column - ratio * its_heads[e]
+                top = top - ratio[one, :] * its_top
+                beside = beside - ratio[one, :] * its_side
+                heads = [
+                    head - ratio[one, :] * its_heads[e + 1 + i]
+                    for i, head in enumerate(heads)
+                ]
+            ratio = jnp.where(one_line > j, column * (1.0 / column[one, :]), 0.0)
+            done.append((ratio, top, beside, heads))
+        for ratio, top, beside, _ in done:
+            rows = rows - ratio * top
+            side = side - ratio * beside
+    if part < TURNS - 1:
+        rest[lines, :] = rows
+        right[lines, :] = side
         return
     diagonal = jnp.sum(
         jnp.where(lane == first + line, rows, 0.0), axis=1, keepdims=True
     )
-    rows = jnp.where(lane >= first + line, rows / jnp.sqrt(diagonal), 0.0)
-    upper[pl.ds(first, block), :] = rows
+    scale = 1.0 / jnp.sqrt(diagonal)
+    rows = jnp.where(lane >= first + line, rows * scale, 0.0)
+    side = side * scale
+    inverse[lines, :] = side
     rest[...] -= tn(rows, rows, HIGH)
-
-
-def start_invert(lower, inverse):
-    i = lax.broadcasted_iota(jnp.int32, lower.shape, 0)
-    j = lax.broadcasted_iota(jnp.int32, lower.shape, 1)
-    inverse[...] = jnp.where(i == j, 1.0 / jnp.where(i == j, lower[...], 1.0), 0.0)
-
-
-def invert_level(k, lower, inverse):
-    i = lax.broadcasted_iota(jnp.int32, lower.shape, 0)
-    j = lax.broadcasted_iota(jnp.int32, lower.shape, 1)
-    i_block, j_block = lax.shift_right_logical(i, k), lax.shift_right_logical(j, k)
-    same = lax.shift_right_logical(i, k + 1) == lax.shift_right_logical(j, k + 1)
-    below = jnp.where(jnp.logical_and(same, i_block > j_block), lower[...], 0.0)
-    right = jnp.dot(below, inverse[...], precision=HIGH, preferred_element_type=F32)
-    inverse[...] -= jnp.dot(inverse[...], right, precision=HIGH, preferred_element_type=F32)
+    right[...] -= tn(rows, side, HIGH)
 
 
 class Ring:
@@ -533,7 +547,7 @@
         return self.tok_of(self.at(1)), self.tok_of(self.at(-1))
 
 
-def ring_scatter(ring, term, store, send, recv, sems):
+def ring_scatter(ring, prepare, term, store, send, recv, sems):
     n = ring.n
     dest = ring.neighbours()
 
@@ -548,6 +562,7 @@
 
     for piece in range(RING_PIECES):
         for way in WAYS:
+            prepare(way, piece)
             send[way, 0, piece] = term(way, piece, block(way, 0)).astype(BF16)
             copy(way, 0, piece).start()
 
@@ -582,6 +597,12 @@
     rows, width = out.shape
     part = width // (2 * RING_PIECES)
 
+    def prepare(way, piece):
+        first = (way * RING_PIECES + piece) * part
+        last = first + part
+        value = tn(proj[...], grads[:, first:last])
+        terms[:, :, first:last] = (value * scale).reshape(place.n, rows, part)
+
     def term(way, piece, pos):
         first = (way * RING_PIECES + piece) * part
         return terms[ring.tok_of(pos), :, first : first + part]
@@ -590,11 +611,7 @@
         first = (way * RING_PIECES + piece) * part
         out[:, first : first + part] = total
 
-    for first in range(0, width, part):
-        last = first + part
-        piece = tn(proj[...], grads[:, first:last])
-        terms[:, :, first:last] = (piece * scale).reshape(place.n, rows, part)
-    ring_scatter(ring, term, store, send, recv, sems)
+    ring_scatter(ring, prepare, term, store, send, recv, sems)
 
 
 def kernel(n, m, scale, names, acts_in, grads_in, test_in, out, *refs):
@@ -630,7 +647,7 @@
         ),
     )
     gather_slot, finish_gather, drain_gather = gather_sketch(
-        place, s.acts, s.full, s.mixed, gram, s.rest, s.lower, s.inverse,
+        place, s.acts, s.full, s.mixed, gram, s.rest, s.right, s.inverse,
         (s.back_send, s.back_recv), (s.forward_send, s.forward_recv),
         (s.swap_send, s.swap_recv),
     )
@@ -692,11 +709,10 @@
         "gram": vmem((rank, rank), F32),
         **pair("gram", (2, m - 1)),
         **pair("gram_x", (1,)),
-        "gram_z_send": dma((LAST,)),
-        "gram_z_recv": dma((ENDS,)),
+        **pair("gram_z", (ENDS,)),
         "mixed": vmem((tokens, rank), F32),
         "rest": vmem((rank, rank), F32),
-        "lower": vmem((rank, rank), F32),
+        "right": vmem((rank, rank), F32),
         "inverse": vmem((rank, rank), F32),
         **pair("back", (ENDS, HOPS)),
         **pair("forward", (ENDS, PIECES)),
@@ -769,7 +785,7 @@
             and rank % (16 * m) == 0
             and rank % (16 * PIECES) == 0
             and rank % (16 * n) == 0
-            and rank <= 512
+            and rank % (PANELS * TURNS * STEP) == 0
             and hidden % (ENDS * 2 * PARTS * 128) == 0
             and model % (2 * RING_PIECES * 128) == 0
             and (tokens * hidden + 2 * rank * hidden) * 2 < VMEM_LIMIT // 2

time: 209 us -> 188 us (0.90)
  Pallas kernels: 207 us -> 186 us
    pallas_call x1, Pallas kernels: 207 us -> 186 us  [line_shards(): pl.pallas_call(functools.partial(kernel, n, m, scale, tuple(scratch)), ou...]
where the time goes in v2:
time: 188 us
  Pallas kernels  186 us (99%)
    pallas_call x1, Pallas kernels, line_shards(): pl.pallas_call(functools.partial(kernel, n, m, scale, tuple(scratch)), ou...  186 us

profile of v2, /device:TPU:0, one launch (start us, length us, event | category | flops | bytes accessed | tf_op | source)
XLA Modules:
  0.0 188.3 jit_solution(10988928985049575250)
XLA Ops:
  0.0 186.4 %shard_map.37 = f32[32,4096]{1,0:T(8,128)} custom-call(bf16[384,13312]{1,0:T(8,128)(2,1)} %acts_in.1, bf16[384,4096]{1,0:T(8,128)(2,1)} %grads_in.1, bf16[4096,256]{1,0:T(8,128)(2,1)} %test_in.1), custom_call_target="tpu_custom_call" | custom-call | tf_op jit(solution)/shard_map/pallas_call | solution.py:736
  186.4 1.9 copy.5

commit v3 on v2

--- a/solution.py
+++ b/solution.py
@@ -22,6 +22,7 @@
 TURNS = 2
 STEP = 8
 GROUPS = 3
+HALVES = 2
 SKEW = 5
 HOPS = GROUPS * PIECES
 LAST = LINE - 1
@@ -256,6 +257,60 @@
     return slot, drain
 
 
+class Projections:
+    def __init__(self, place, mixed, got, totals, mine, proj, inverse, sems):
+        self.place, self.mixed, self.got, self.totals = place, mixed, got, totals
+        self.mine, self.proj, self.inverse, self.sems = mine, proj, inverse, sems
+        self.lines = shares(place, mixed.shape[1])
+        self.peers = range(1, place.m)
+
+    def first(self, half, k):
+        other = self.place.peer(k)
+        return remote(
+            self.mixed.at[half, self.lines(other)], self.got.at[half, k - 1], self.sems,
+            (0, half, k - 1), {"wid": other},
+        )
+
+    def second(self, half, k):
+        return remote(
+            self.mine.at[half], self.proj.at[half, self.lines(self.place.wid)], self.sems,
+            (1, half, k - 1), {"wid": self.place.peer(k)},
+        )
+
+    def start(self, half):
+        for k in self.peers:
+            self.first(half, k).start()
+
+    def spread(self, half):
+        total = self.mixed[half, self.lines(self.place.wid), :]
+        for k in self.peers:
+            self.first(half, k).wait_recv()
+            total = total + self.got[half, k - 1]
+        self.totals[half] = total
+        size = total.shape[1]
+        lines = slice(half * size, (half + 1) * size)
+        value = jnp.zeros_like(total)
+        for h in range(half + 1):
+            block = self.inverse[lines, h * size : (h + 1) * size]
+            value = value + nt(self.totals[h], block, HIGH)
+        value = value.astype(self.mine.dtype)
+        self.mine[half] = value
+        for k in self.peers:
+            self.second(half, k).start()
+        self.proj[half, self.lines(self.place.wid), :] = value
+
+    def finish(self):
+        for half in range(HALVES):
+            for k in self.peers:
+                self.second(half, k).wait_recv()
+
+    def drain(self):
+        for half in range(HALVES):
+            for k in self.peers:
+                self.first(half, k).wait_send()
+                self.second(half, k).wait_send()
+
+
 class Gram:
     def __init__(self, place, part, got, share, crossed, ends, mine, gram, sems):
         self.place, self.part, self.got, self.share = place, part, got, share
@@ -350,13 +405,16 @@
             self.spread(k).wait_send()
 
 
-def gather_sketch(place, acts, full, mixed, gram, rest, right, inverse, line_sems, forward_sems, swap_sems):
+def gather_sketch(place, acts, full, sums, gram, rest, right, inverse, line_sems, forward_sems, swap_sems):
     x, end = place.x, place.end
     rank, width = rest.shape[0], full.shape[-1]
+    mixed, run = sums.mixed, PIECES // HALVES
+    per_half = GROUPS * run
     solve_at = FILL + 29
 
     def spot(end_, k):
-        group, piece = lax.div(k, PIECES), lax.rem(k, PIECES)
+        half, rest_of = lax.div(k, per_half), lax.rem(k, per_half)
+        group, piece = lax.div(rest_of, run), half * run + lax.rem(rest_of, run)
         side = jnp.where(group == GROUPS - 1, 1 - x, x)
         part = jnp.where(group == 0, 0, 1)
         return group, piece, unit_of(end_, side, part)
@@ -391,9 +449,19 @@
         def _():
             line_copy(way, k).start()
 
-    def add(unit):
+    def add(half, unit):
         columns = pl.ds(pl.multiple_of(unit * width, 128), width)
-        mixed[...] += nt(acts[:, columns], full[unit].reshape(rank, width))
+        block = full[unit, half * run : (half + 1) * run]
+        mixed[half] += nt(acts[:, columns], block.reshape(rank // HALVES, width))
+
+    adds = []
+    for half in range(HALVES):
+        for way in WAYS:
+            ready = half * per_half + FILL + way
+            adds.append((ready + run, half, unit_of(way, x, 0)))
+            adds.append((ready + 2 * run, half, unit_of(way, x, 1)))
+            adds.append((ready + 3 * run, half, unit_of(way, 1 - x, 1)))
+            adds.append((ready + (way + 2) * run + 2, half, unit_of(way, 1 - x, 0)))
 
     mixed[...] = jnp.zeros_like(mixed)
 
@@ -405,10 +473,13 @@
         for way in WAYS:
             k = s - SKEW * place.to_end(1 - way)
             pl.when(within(k, 0, HOPS))(functools.partial(hop, way, k))
-            sent = s - FILL - way * PIECES
-            pl.when(within(sent, 0, PIECES))(lambda: forward_copy(way, sent).start())
-            came = sent - 12
-            pl.when(within(came, 0, PIECES))(lambda: forward_copy(way, came).wait_recv())
+            for half in range(HALVES):
+                sent = s - FILL - half * per_half - way * run
+                piece = half * run + sent
+                pl.when(within(sent, 0, run))(lambda: forward_copy(way, piece).start())
+                pl.when(within(sent, run, run))(
+                    lambda: forward_copy(way, piece - run).wait_recv()
+                )
 
         pl.when(s == FILL)(lambda: gram.start(full))
         pl.when(s == FILL + 4)(gram.cross)
@@ -429,14 +500,19 @@
                 lambda: solve_part(lax.div(solve, TURNS), part, rest, right, inverse)
             )
 
-        for way in WAYS:
-            pl.when(s == PIECES + FILL + way)(lambda: add(unit_of(way, x, 0)))
-            pl.when(s == 2 * PIECES + FILL + way)(lambda: add(unit_of(way, x, 1)))
-            pl.when(s == (way + 1) * PIECES + FILL + 12)(lambda: add(unit_of(way, 1 - x, 0)))
+        for at, half, unit in adds:
+            if at < HOPS + FILL:
+                pl.when(s == at)(lambda: add(half, unit))
+        pl.when(s == FILL + per_half + 4)(lambda: sums.start(0))
+        pl.when(s == solve_at + TURNS * PANELS // HALVES + 2)(lambda: sums.spread(0))
 
     def finish():
-        for way in WAYS:
-            add(unit_of(way, 1 - x, 1))
+        for at, half, unit in adds:
+            if at >= HOPS + FILL:
+                add(half, unit)
+        sums.start(1)
+        sums.spread(1)
+        sums.finish()
 
     def drain():
         for way in WAYS:
@@ -600,8 +676,11 @@
     def prepare(way, piece):
         first = (way * RING_PIECES + piece) * part
         last = first + part
-        value = tn(proj[...], grads[:, first:last])
-        terms[:, :, first:last] = (value * scale).reshape(place.n, rows, part)
+        count = place.n // HALVES
+        for half in range(HALVES):
+            value = tn(proj[half], grads[:, first:last])
+            blocks = slice(half * count, (half + 1) * count)
+            terms[blocks, :, first:last] = (value * scale).reshape(count, rows, part)
 
     def term(way, piece, pos):
         first = (way * RING_PIECES + piece) * part
@@ -646,8 +725,12 @@
             (s.gram_z_send, s.gram_z_recv),
         ),
     )
+    sums = Projections(
+        place, s.mixed, s.mixed_got, s.mixed_totals, s.proj_mine, s.proj, s.inverse,
+        (s.mixed_send, s.mixed_recv),
+    )
     gather_slot, finish_gather, drain_gather = gather_sketch(
-        place, s.acts, s.full, s.mixed, gram, s.rest, s.right, s.inverse,
+        place, s.acts, s.full, sums, gram, s.rest, s.right, s.inverse,
         (s.back_send, s.back_recv), (s.forward_send, s.forward_recv),
         (s.swap_send, s.swap_recv),
     )
@@ -659,10 +742,6 @@
 
     lax.fori_loop(0, SLOTS, slot, 0)
     finish_gather()
-    wid_sum(
-        place, s.mixed, s.mixed_got, s.proj_mine, s.proj, (s.mixed_send, s.mixed_recv),
-        lambda total: nt(total, s.inverse[...], HIGH),
-    )
     coeffs(
         place, s.proj, s.grads, out, s.out_terms, s.ring_from, s.ring_to,
         (s.ring_send, s.ring_recv), scale,
@@ -670,6 +749,7 @@
     drain_reduce()
     drain_gather()
     gram.drain()
+    sums.drain()
 
 
 def scratch_of(n, m, tokens, hidden, rank, model):
@@ -710,17 +790,18 @@
         **pair("gram", (2, m - 1)),
         **pair("gram_x", (1,)),
         **pair("gram_z", (ENDS,)),
-        "mixed": vmem((tokens, rank), F32),
+        "mixed": vmem((HALVES, tokens, rank // HALVES), F32),
         "rest": vmem((rank, rank), F32),
         "right": vmem((rank, rank), F32),
         "inverse": vmem((rank, rank), F32),
         **pair("back", (ENDS, HOPS)),
         **pair("forward", (ENDS, PIECES)),
         **pair("swap", (PIECES,)),
-        "mixed_got": vmem((m - 1, tokens // m, rank), F32),
-        "proj_mine": vmem((tokens // m, rank), BF16),
-        "proj": vmem((tokens, rank), BF16),
-        **pair("mixed", (2, m - 1)),
+        "mixed_got": vmem((HALVES, m - 1, tokens // m, rank // HALVES), F32),
+        "mixed_totals": vmem((HALVES, tokens // m, rank // HALVES), F32),
+        "proj_mine": vmem((HALVES, tokens // m, rank // HALVES), BF16),
+        "proj": vmem((HALVES, tokens, rank // HALVES), BF16),
+        **pair("mixed", (2, HALVES, m - 1)),
         "out_terms": vmem((n, rows, model), F32),
         "ring_from": vmem((2, n - 1, RING_PIECES, rows, part), BF16),
         "ring_to": vmem((2, n - 1, RING_PIECES, rows, part), BF16),
@@ -786,6 +867,7 @@
             and rank % (16 * PIECES) == 0
             and rank % (16 * n) == 0
             and rank % (PANELS * TURNS * STEP) == 0
+            and rank % (HALVES * 128) == 0
             and hidden % (ENDS * 2 * PARTS * 128) == 0
             and model % (2 * RING_PIECES * 128) == 0
             and (tokens * hidden + 2 * rank * hidden) * 2 < VMEM_LIMIT // 2

time: 188 us -> 188 us (level)
  no operation moved by 1% of the time
where the time goes in v3:
time: 188 us
  Pallas kernels  186 us (99%)
    pallas_call x1, Pallas kernels, line_shards(): pl.pallas_call(functools.partial(kernel, n, m, scale, tuple(scratch)), ou...  186 us

profile of v3, /device:TPU:0, one launch (start us, length us, event | category | flops | bytes accessed | tf_op | source)
XLA Modules:
  0.0 188.1 jit_solution(5795415932562161403)
XLA Ops:
  0.0 186.2 %shard_map.37 = f32[32,4096]{1,0:T(8,128)} custom-call(bf16[384,13312]{1,0:T(8,128)(2,1)} %acts_in.1, bf16[384,4096]{1,0:T(8,128)(2,1)} %grads_in.1, bf16[4096,256]{1,0:T(8,128)(2,1)} %test_in.1), custom_call_target="tpu_custom_call" | custom-call | tf_op jit(solution)/shard_map/pallas_call | solution.py:817
  186.2 1.9 copy.5

commit v4 on v3

--- a/solution.py
+++ b/solution.py
@@ -702,11 +702,12 @@
             ((grads_in, s.grads), (test_in, s.test), (acts_in, s.acts))
         )
     ]
-    for load in loads:
+    for load in loads[:2]:
         load.start()
     place.barrier()
-    loads[0].wait()
-    loads[1].wait()
+    for load in loads[:2]:
+        load.wait()
+    loads[2].start()
     s.probe_part[...] = jnp.dot(s.grads[...], s.test[...], preferred_element_type=F32).T
     wid_sum(
         place, s.probe_part, s.probe_got, s.probe_mine, s.probe,

time: 188 us -> 188 us (level)
  no operation moved by 1% of the time
where the time goes in v4:
time: 188 us
  Pallas kernels  186 us (99%)
    pallas_call x1, Pallas kernels, line_shards(): pl.pallas_call(functools.partial(kernel, n, m, scale, tuple(scratch)), ou...  186 us

profile of v4, /device:TPU:0, one launch (start us, length us, event | category | flops | bytes accessed | tf_op | source)
XLA Modules:
  0.0 188.1 jit_solution(9501553817381950351)
XLA Ops:
  0.0 186.2 %shard_map.37 = f32[32,4096]{1,0:T(8,128)} custom-call(bf16[384,13312]{1,0:T(8,128)(2,1)} %acts_in.1, bf16[384,4096]{1,0:T(8,128)(2,1)} %grads_in.1, bf16[4096,256]{1,0:T(8,128)(2,1)} %test_in.1), custom_call_target="tpu_custom_call" | custom-call | tf_op jit(solution)/shard_map/pallas_call | solution.py:818
  186.2 1.9 copy.5
